TPU v7x, 32 devices: a whole 2x2x4 slice. The times are simulated.
32 devices in a mesh: members: 2 (over y), lat: 4 (over z), lon: 2 (over x), lev: 2 (over core).
Axes of the slice: x: 2, y: 2, z: 4, core: 2. Of those that a mesh axis runs over, the one named last changes fastest.
Arguments:
- wind_east: float32 [8, 360, 2880], P(('members', 'lev'), 'lat', 'lon'), parts along dimension 0, may hold values from -6 to 6
- wind_north: float32 [8, 360, 2880], P(('members', 'lev'), 'lat', 'lon'), parts along dimension 0, may hold values from -6 to 6
- thickness: float32 [8, 360, 2880], P(('members', 'lev'), 'lat', 'lon'), parts along dimension 0, may hold values from -6 to 6
- geopot: float32 [8, 360, 2880], P(('members', 'lev'), 'lat', 'lon'), parts along dimension 0, may hold values from -6 to 6
- surface_geopot: float32 [360, 2880], P('lat', 'lon'), may hold values from -6 to 6
- mean_depth: float32 [4], P('lev'), may hold values from 0.5 to 2
- kept_modes: int32 [180], replicated, may hold values from 1 to 360
- slot_table: int32 [180], replicated, may hold values from 0 to 179, as said below
Outputs:
- east_final: float32 [8, 360, 2880], P(('members', 'lev'), 'lat', 'lon'), parts along dimension 0
- north_final: float32 [8, 360, 2880], P(('members', 'lev'), 'lat', 'lon'), parts along dimension 0
- thick_new: float32 [8, 360, 2880], P(('members', 'lev'), 'lat', 'lon'), parts along dimension 0
- geo_new: float32 [8, 360, 2880], P(('members', 'lev'), 'lat', 'lon'), parts along dimension 0
- spectra: float32 [2, 8, 180, 720], P(None, ('members', 'lev'), 'lat', 'lon'), parts along dimension 1
There are 2 independent parts, one for each index of `members`. A program takes and returns all parts, laid end to end along the dimension named above; an argument that names none is the same for every part. Nothing has to cross between parts.
Inputs may be any that keep to these rules, and one draw needn't show every extreme that they name: `slot_table`: every slot 0 to 179 is named once; slot s belongs to latitude device s // 45. Of the 90 polar rows held by latitude device d, 45 name slots of device d and 45 name slots of the device half the lat axis away, (d + 4 / 2) mod 4.
All inputs are finite; a program needn't handle non-finite values.
Results may differ from a plain program's by a relative error of at most 0.00019.
Values sent between devices are 32-bit elements; how exact they have to be, the bound alone decides.
A program may use at most 64 MiB of HBM per device.

v0:
```python
import math

import jax
import numpy as np
import jax.numpy as jnp
from jax import lax
from jax.sharding import PartitionSpec as P

KMAX = 360


STEP_FACTOR = 0.15
CORIOLIS = 0.2
GRAVITY = 0.25


def edges(block, axis, dim, periodic):
    count = lax.axis_size(axis)
    first = lax.slice_in_dim(block, 0, 1, axis=dim)
    last = lax.slice_in_dim(block, block.shape[dim] - 1, block.shape[dim], axis=dim)
    if periodic and count == 2:
        both = lax.ppermute(jnp.concatenate([last, first], axis=dim), axis, [(0, 1), (1, 0)])
        return lax.slice_in_dim(both, 0, 1, axis=dim), lax.slice_in_dim(both, 1, 2, axis=dim)
    forward = [(i, i + 1) for i in range(count - 1)]
    if periodic:
        forward.append((count - 1, 0))
    backward = [(target, source) for source, target in forward]
    return lax.ppermute(last, axis, forward), lax.ppermute(first, axis, backward)


def diff(block, low, high, dim):
    size = block.shape[dim]
    up = jnp.concatenate([lax.slice_in_dim(block, 1, size, axis=dim), high], axis=dim)
    down = jnp.concatenate([low, lax.slice_in_dim(block, 0, size - 1, axis=dim)], axis=dim)
    return up - down


def local_basis(count, nlon_total):
    fine = next(f for f in (24, 20, 18, 16, 12, 8, 6, 5, 4, 3, 2, 1) if count % f == 0)
    k = np.arange(KMAX, dtype=np.int64)[None, :]
    angle = 2.0 * np.pi / nlon_total

    def table(columns):
        phase = (columns[:, None] * k % nlon_total) * angle
        return np.cos(phase).astype(np.float32), np.sin(phase).astype(np.float32)

    cc, cs = (jnp.asarray(t)[:, None] for t in table(np.arange(0, count, fine)))
    fc, fs = (jnp.asarray(t)[None] for t in table(np.arange(fine)))
    return (
        (cc * fc - cs * fs).reshape(count, KMAX),
        (cs * fc + cc * fs).reshape(count, KMAX),
    )


def turned(pair, cos_shift, sin_shift):
    cos_part, sin_part = pair[..., :KMAX], pair[..., KMAX:]
    return jnp.concatenate(
        [cos_shift * cos_part - sin_shift * sin_part, sin_shift * cos_part + cos_shift * sin_part],
        axis=-1,
    )


def local(
    wind_east, wind_north, thickness, geopot, surface_geopot, mean_depth, kept_modes, slot_table
):
    lev_dev, lat_dev, lon_dev = thickness.shape
    lat_count = lax.axis_size("lat")
    lon_count = lax.axis_size("lon")
    lev_count = lax.axis_size("lev")
    lat_index = lax.axis_index("lat")
    lon_index = lax.axis_index("lon")
    nlat_total = lat_dev * lat_count
    nlon_total = lon_dev * lon_count
    polar_count = nlat_total // 4
    slot_count = 2 * polar_count
    help_rows = lat_dev // 2
    half_axis = lat_count // 2
    lam_step = 2.0 * math.pi / nlon_total
    phi_step = math.pi / nlat_total
    global_rows = lat_index * lat_dev + jnp.arange(lat_dev, dtype=jnp.int32)
    latitude = -0.5 * math.pi + (global_rows.astype(jnp.float32) + 0.5) * phi_step
    coslat = jnp.cos(latitude)[:, None]
    sinlat = jnp.sin(latitude)[:, None]
    east_coef = STEP_FACTOR / coslat
    north_coef = STEP_FACTOR * lam_step / phi_step
    geo_west, geo_east = edges(geopot, "lon", 2, True)
    geo_south, geo_north = edges(geopot, "lat", 1, False)
    east_new = (
        wind_east
        - east_coef * diff(geopot, geo_west, geo_east, 2)
        + CORIOLIS * sinlat * wind_north
    )
    north_new = (
        wind_north
        - north_coef * diff(geopot, geo_south, geo_north, 1)
        - CORIOLIS * sinlat * wind_east
    )
    is_polar = (lat_index < lat_count // 4) | (lat_index >= lat_count - lat_count // 4)
    first_row = lat_index * lat_dev
    first_rank = jnp.where(lat_index < lat_count // 4, first_row, first_row - (nlat_total - slot_count))
    first_rank = jnp.clip(first_rank, 0, slot_count - lat_dev)
    kept = lax.dynamic_slice(kept_modes, (first_rank,), (lat_dev,))
    slots = lax.dynamic_slice(slot_table, (first_rank,), (lat_dev,))
    wavenumber = jnp.arange(2 * KMAX, dtype=jnp.int32) % KMAX
    weight = (jnp.where(wavenumber == 0, 1.0, 2.0) / nlon_total).astype(jnp.float32)
    factor = jnp.where(wavenumber[None, :] < kept[:, None], weight[None, :], 0.0)
    cos_basis, sin_basis = local_basis(lon_dev, nlon_total)
    basis = jnp.concatenate([cos_basis, sin_basis], axis=1)
    shift = (lon_index * jnp.arange(KMAX, dtype=jnp.int32) % lon_count).astype(jnp.float32)
    shift = shift * (2.0 * math.pi / lon_count)
    if lon_count == 2:
        cos_shift = 1.0 - 2.0 * (lon_index * jnp.arange(KMAX, dtype=jnp.int32) % 2).astype(jnp.float32)
        sin_shift = jnp.zeros_like(cos_shift)
    else:
        cos_shift, sin_shift = jnp.cos(shift), jnp.sin(shift)
    pieces = [wind[level] for level in range(lev_dev) for wind in (east_new, north_new)]
    both_sums = []
    for piece in range(lev_dev):
        rows = jnp.concatenate(pieces[2 * piece : 2 * piece + 2], axis=0)
        part = jnp.dot(rows, basis, precision=lax.Precision.HIGH)
        part = turned(part, cos_shift, sin_shift)
        if lon_count == 2:
            sums = part + lax.ppermute(part, "lon", [(0, 1), (1, 0)])
        else:
            sums = lax.psum(part, "lon")
        both_sums.append(sums.reshape(2, lat_dev, 2 * KMAX) * factor[None])
    filtered = []
    for sums in both_sums:
        turned_back = turned(sums, cos_shift, -sin_shift)
        rows = lax.dot_general(
            turned_back.reshape(2 * lat_dev, 2 * KMAX),
            basis,
            (((1,), (1,)), ((), ())),
            precision=lax.Precision.HIGH,
        )
        filtered.append(rows.reshape(2, lat_dev, lon_dev))
    filtered = jnp.stack(filtered, axis=1)
    east_final = jnp.where(is_polar, filtered[0], east_new)
    north_final = jnp.where(is_polar, filtered[1], north_new)

    slice_width = 2 * KMAX // lon_count
    kept_sums = jnp.stack(both_sums, axis=1)
    own = lax.dynamic_slice_in_dim(kept_sums, lon_index * slice_width, slice_width, 3)
    places = jnp.arange(help_rows, dtype=jnp.int32)
    partner = (lat_index + half_axis) % lat_count

    def rows_named(device):
        match = slots[None, :] == (device * help_rows + places)[:, None]
        return jnp.einsum(
            "sr,abrc->absc", match.astype(jnp.float32), own, precision=lax.Precision.HIGHEST
        )

    route = [((i - half_axis) % lat_count, i) for i in range(lat_count)]
    route = [(s, t) for s, t in route if s < lat_count // 4 or s >= lat_count - lat_count // 4]
    arrived = lax.ppermute(rows_named(partner), "lat", route)
    spectra = jnp.where(is_polar, rows_named(lat_index), arrived)

    rim_west, rim_east = edges(east_final, "lon", 2, True)
    flux = north_final * coslat
    rim_south, rim_north = edges(flux, "lat", 1, False)
    divergence = east_coef * diff(east_final, rim_west, rim_east, 2) + north_coef / coslat * diff(
        flux, rim_south, rim_north, 1
    )
    thick_new = thickness - mean_depth[:, None, None] * divergence
    columns = [thick_new[lev_dev - 1]]
    for level in range(lev_dev - 2, -1, -1):
        columns.append(columns[-1] + thick_new[level])
    columns = columns[::-1]
    deeper = jnp.zeros_like(columns[0])
    for distance in range(1, lev_count):
        deeper = deeper + lax.ppermute(
            columns[0], "lev", [(i + distance, i) for i in range(lev_count - distance)]
        )
    geo_new = surface_geopot[None] + GRAVITY * (jnp.stack(columns) + deeper[None])
    return (east_final, north_final, thick_new, geo_new, spectra)


def solution(mesh):
    return jax.shard_map(
        local,
        mesh=mesh,
        in_specs=(
            P(("members", "lev"), "lat", "lon"),
            P(("members", "lev"), "lat", "lon"),
            P(("members", "lev"), "lat", "lon"),
            P(("members", "lev"), "lat", "lon"),
            P("lat", "lon"),
            P("lev"),
            P(),
            P(),
        ),
        out_specs=(
            P(("members", "lev"), "lat", "lon"),
            P(("members", "lev"), "lat", "lon"),
            P(("members", "lev"), "lat", "lon"),
            P(("members", "lev"), "lat", "lon"),
            P(None, ("members", "lev"), "lat", "lon"),
        ),
        check_vma=False,
    )
```

profile of v0, /device:TPU:15, one launch (start us, length us, event | category | flops | bytes accessed | tf_op | source)
XLA Modules:
  0.0 109.9 jit_solution(1433863506138340073)
XLA Ops:
  3.7 2.1 %collective-permute-start.1 = (f32[2,1,1440]{2,1,0:T(1,128)}, f32[2,1,1440]{2,1,0:T(1,128)}, u32[]{:S(2)}, u32[]{:S(2)}) collective-permute-start(f32[2,1,1440]{2,1,0:T(1,128)} %copy.92), channel_id=1, source_target_pairs={{4,0},{8,4},{12,8},{5,1},{9,5},{13,9},{6,2},{10,6},{14,10},{7,3},{... | collective-permute-start | bytes 34568 | tf_op jit(solution)/shard_map/ppermute | solution.py:28
  6.4 3.2 %collective-permute-start.2 = (f32[2,1,1440]{2,1,0:T(1,128)}, f32[2,1,1440]{2,1,0:T(1,128)}, u32[]{:S(2)}, u32[]{:S(2)}) collective-permute-start(f32[2,1,1440]{2,1,0:T(1,128)} %copy.93), channel_id=1, source_target_pairs={{0,4},{4,8},{8,12},{1,5},{5,9},{9,13},{2,6},{6,10},{10,14},{3,7},{... | collective-permute-start | bytes 34568 | tf_op jit(solution)/shard_map/ppermute | solution.py:28
  9.6 3.9 %fusion.79 = (f32[2,90,1439]{2,0,1:T(2,128)S(1)}, f32[2,90,1439]{2,0,1:T(2,128)}) fusion(f32[2,90,1440]{2,0,1:T(2,128)} %param.15), kind=kLoop, calls=%fused_computation.122 | loop fusion | bytes 4144320 | tf_op jit(solution)/shard_map/slice | solution.py:34
  13.6 1.9 %fusion.78 = (f32[2,89,1440]{2,0,1:T(2,128)}, f32[2,89,1440]{2,0,1:T(2,128)}) fusion(f32[2,90,1440]{2,0,1:T(2,128)S(1)} %copy-done.2), kind=kLoop, calls=%fused_computation.121 | loop fusion | bytes 4101120 | tf_op jit(solution)/shard_map/slice | solution.py:34
  17.3 1.6 %multiply_subtract_fusion = (f32[60,24,360]{2,1,0:T(8,128)S(1)}, f32[60,24,360]{2,1,0:T(8,128)S(1)}) fusion(f32[24,360]{1,0:T(8,128)} %constant.103.clone, f32[60,360]{1,0:T(8,128)} %constant.101.clone, f32[24,360]{1,0:T(8,128)S(1)} %copy-done.19, f32[60,360]{1,0:T(8,128)} %constant.100.clone), kind=kLoop, calls=%fused_computation.10 | loop fusion | flops 3110400 | bytes 4389120 | tf_op jit(solution)/shard_map/sub | solution.py:50
  19.4 1.5 %copy-done.8 = f32[2,89,1440]{2,0,1:T(2,128)S(1)} copy-done((f32[2,89,1440]{2,0,1:T(2,128)S(1)}, f32[2,89,1440]{2,0,1:T(2,128)}, u32[]{:S(2)}) %copy-start.8) | copy-done | bytes 1025304
  22.8 1.7 %fusion.22 = (f32[2,90,1440]{2,1,0:T(8,128)S(1)}, f32[2,90,1440]{2,1,0:T(8,128)S(1)}) fusion(f32[2,1,1440]{2,1,0:T(1,128)} %collective-permute-done.1, f32[2,89,1440]{2,1,0:T(8,128)S(1)} %copy.112, f32[2,89,1440]{2,1,0:T(8,128)S(1)} %copy.113, f32[2,1,1440]{2,1,0:T(1,128)} %collective-permute-done.2, f32[2,90,1440]{2,0,1:T(2,128)S(1)} %copy-done.16, ...), kind=kLoop, calls=%fused_computation.26 | loop fusion | flops 3628800 | bytes 8295120 | tf_op jit(solution)/shard_map/sub | solution.py:94
  25.6 2.2 %fusion.11 = f32[180,720]{1,0:T(8,128)S(1)} fusion(f32[1440,360]{1,0:T(8,128)S(1)} %bitcast.59, f32[1440,360]{1,0:T(8,128)S(1)} %bitcast.55, f32[90,1440]{1,0:T(8,128)S(1)} %get-tuple-element.43, f32[90,1440]{1,0:T(8,128)S(1)} %get-tuple-element.41), kind=kOutput, calls=%fused_computation.12 | convolution fusion | flops 1121040000 | bytes 5702400 | tf_op jit(solution)/shard_map/dot_general | solution.py:120
  27.9 2.2 %fusion.10 = f32[180,720]{1,0:T(8,128)S(1)} fusion(f32[1440,360]{1,0:T(8,128)S(1)} %bitcast.60, f32[1440,360]{1,0:T(8,128)S(1)} %bitcast.56, f32[90,1440]{1,0:T(8,128)S(1)} %get-tuple-element.42, f32[90,1440]{1,0:T(8,128)S(1)} %get-tuple-element.40), kind=kOutput, calls=%fused_computation.11 | convolution fusion | flops 1121040000 | bytes 5702400 | tf_op jit(solution)/shard_map/dot_general | solution.py:120
  34.5 2.0 %pad_maximum_fusion.7 = f32[180,720]{1,0:T(8,128)} fusion(f32[180,360]{1,0:T(8,128)} %get-tuple-element.57, f32[180,360]{1,0:T(8,128)} %get-tuple-element.56), kind=kLoop, calls=%fused_computation.64 | loop fusion | flops 129600 | bytes 1036800 | tf_op jit(solution)/shard_map/concatenate | solution.py:57
  38.4 7.6 %collective-permute-done.3 = f32[180,720]{1,0:T(8,128)} collective-permute-done((f32[180,720]{1,0:T(8,128)}, f32[180,720]{1,0:T(8,128)}, u32[]{:S(2)}, u32[]{:S(2)}) %collective-permute-start.3) | collective-permute-done | bytes 518432 | tf_op jit(solution)/shard_map/ppermute | solution.py:123
  45.9 2.2 %fusion.71 = f32[180,720]{1,0:T(8,128)} fusion(f32[180,720]{1,0:T(8,128)} %collective-permute-done.3, f32[180,360]{1,0:T(8,128)} %copy-done.10, f32[180,360]{1,0:T(8,128)} %copy-done.11), kind=kLoop, calls=%fused_computation.115 | loop fusion | flops 259200 | bytes 1555200 | tf_op jit(solution)/shard_map/add | solution.py:123
  48.1 1.9 %reshape.203 = f32[2,1,90,720]{3,2,0,1:T(8,128)} reshape(f32[180,720]{1,0:T(8,128)} %fusion.71) | data formatting | bytes 1036800 | tf_op jit(solution)/shard_map/reshape | solution.py:126
  50.0 1.9 %reshape.201 = f32[2,90,720]{2,1,0:T(8,128)} reshape(f32[180,720]{1,0:T(8,128)} %fusion.71) | data formatting | bytes 1036800 | tf_op jit(solution)/shard_map/reshape | solution.py:126
  52.0 6.1 %collective-permute-done.4 = f32[180,720]{1,0:T(8,128)} collective-permute-done((f32[180,720]{1,0:T(8,128)}, f32[180,720]{1,0:T(8,128)}, u32[]{:S(2)}, u32[]{:S(2)}) %collective-permute-start.4) | collective-permute-done | bytes 518432 | tf_op jit(solution)/shard_map/ppermute | solution.py:123
  58.0 2.2 %fusion.70 = f32[180,720]{1,0:T(8,128)} fusion(f32[180,720]{1,0:T(8,128)} %collective-permute-done.4, f32[180,360]{1,0:T(8,128)} %get-tuple-element.57, f32[180,360]{1,0:T(8,128)} %get-tuple-element.56), kind=kLoop, calls=%fused_computation.114 | loop fusion | flops 259200 | bytes 1555200 | tf_op jit(solution)/shard_map/add | solution.py:123
  60.2 1.9 %reshape.204 = f32[2,1,90,720]{3,2,0,1:T(8,128)} reshape(f32[180,720]{1,0:T(8,128)} %fusion.70) | data formatting | bytes 1036800 | tf_op jit(solution)/shard_map/reshape | solution.py:126
  62.2 1.9 %reshape.202 = f32[2,90,720]{2,1,0:T(8,128)} reshape(f32[180,720]{1,0:T(8,128)} %fusion.70) | data formatting | bytes 1036800 | tf_op jit(solution)/shard_map/reshape | solution.py:126
  64.1 1.4 %broadcast_multiply_fusion.1 = (f32[2,90,720]{2,1,0:T(8,128)S(1)}, f32[2,90,720]{2,1,0:T(8,128)S(1)}) fusion(f32[2,90,720]{2,1,0:T(8,128)} %reshape.202, f32[90,720]{1,0:T(8,128)} %compare_select_fusion, f32[2,90,720]{2,1,0:T(8,128)} %reshape.201), kind=kLoop, calls=%fused_computation.69 | loop fusion | flops 259200 | bytes 2332800 | tf_op jit(solution)/shard_map/mul | solution.py:126
  67.2 2.7 %fusion.4 = f32[2,1,90,1440]{3,2,0,1:T(8,128)S(1)} fusion(f32[1440,360]{1,0:T(8,128)S(1)} %bitcast.61, f32[1440,360]{1,0:T(8,128)S(1)} %bitcast.57, f32[2,90,360]{2,1,0:T(8,128)S(1)} %get-tuple-element.70, f32[2,90,360]{2,1,0:T(8,128)S(1)} %get-tuple-element.71), kind=kOutput, calls=%fused_computation.5 | convolution fusion | flops 1120910336 | bytes 5702400 | tf_op jit(solution)/shard_map/dot_general | solution.py:130
  69.8 2.5 %fusion.7 = f32[2,1,90,1440]{3,2,0,1:T(8,128)S(1)} fusion(f32[1440,360]{1,0:T(8,128)S(1)} %bitcast.62, f32[1440,360]{1,0:T(8,128)S(1)} %bitcast.58, f32[2,90,360]{2,1,0:T(8,128)S(1)} %get-tuple-element.53, f32[2,90,360]{2,1,0:T(8,128)S(1)} %get-tuple-element.52), kind=kOutput, calls=%fused_computation.6 | convolution fusion | flops 1120910336 | bytes 5702400 | tf_op jit(solution)/shard_map/dot_general | solution.py:130
  72.3 1.6 %broadcast_multiply_fusion = (f32[2,90,1440]{2,1,0:T(8,128)S(1)}, f32[2,90,1440]{2,1,0:T(8,128)}, f32[2,90,1440]{2,1,0:T(8,128)S(1)}) fusion(f32[90]{0:T(128)S(1)} %fusion.63, f32[2,90,1440]{2,1,0:T(8,128)S(1)} %get-tuple-element.28, f32[2,1,90,1440]{3,2,0,1:T(8,128)S(1)} %fusion.7, f32[2,1,90,1440]{3,2,0,1:T(8,128)S(1)} %fusion.4, pred[]{:T(512)S(6)} %or.3, ...), kind=kLoop, calls=%fused_computation.62 | loop fusion | flops 1296000 | bytes 7257961 | tf_op jit(solution)/shard_map/mul | solution.py:159
  76.1 2.6 %collective-permute-start.6 = (f32[2,1,1440]{2,1,0:T(1,128)S(1)}, f32[2,1,1440]{2,1,0:T(1,128)S(1)}, u32[]{:S(2)}, u32[]{:S(2)}) collective-permute-start(f32[2,1,1440]{2,1,0:T(1,128)S(1)} %get-tuple-element.33), channel_id=1, source_target_pairs={{4,0},{8,4},{12,8},{5,1},{9,5},{13,9},{6,2},{10,6},{14,10},{7,3},{... | collective-permute-start | bytes 34568 | tf_op jit(solution)/shard_map/ppermute | solution.py:28
  78.8 3.2 %collective-permute-start.7 = (f32[2,1,1440]{2,1,0:T(1,128)S(1)}, f32[2,1,1440]{2,1,0:T(1,128)S(1)}, u32[]{:S(2)}, u32[]{:S(2)}) collective-permute-start(f32[2,1,1440]{2,1,0:T(1,128)S(1)} %get-tuple-element.32), channel_id=1, source_target_pairs={{0,4},{4,8},{8,12},{1,5},{5,9},{9,13},{2,6},{6,10},{10,14},{3,7},{... | collective-permute-start | bytes 34568 | tf_op jit(solution)/shard_map/ppermute | solution.py:28
  85.3 6.8 %collective-permute-start.8 = (f32[90,1440]{1,0:T(8,128)}, f32[90,1440]{1,0:T(8,128)}, u32[]{:S(2)}, u32[]{:S(2)}) collective-permute-start(f32[90,1440]{1,0:T(8,128)} %bitcast.11), channel_id=1, source_target_pairs={{1,0},{3,2},{5,4},{7,6},{9,8},{11,10},{13,12},{15,14},{17,16},{19,... | collective-permute-start | bytes 1555208 | tf_op jit(solution)/shard_map/ppermute | solution.py:171
  94.7 1.8 %copy.101 = f32[2,90,1440]{2,0,1:T(2,128)} copy(f32[2,90,1440]{2,1,0:T(8,128)S(1)} %get-tuple-element.27) | data formatting | bytes 2073600
  96.5 1.8 %copy.102 = f32[2,90,1440]{2,0,1:T(2,128)} copy(f32[2,90,1440]{2,1,0:T(8,128)S(1)} %copy-done.5) | data formatting | bytes 2073600
  98.4 1.8 %copy.103 = f32[2,90,1440]{2,0,1:T(2,128)} copy(f32[2,90,1440]{2,1,0:T(8,128)S(1)} %fusion.26) | data formatting | bytes 2073600
  100.2 4.0 %collective-permute-done.9 = f32[2,2,45,360]{3,2,1,0:T(8,128)} collective-permute-done((f32[2,2,45,360]{3,2,1,0:T(8,128)}, f32[2,2,45,360]{3,2,1,0:T(8,128)}, u32[]{:S(2)}, u32[]{:S(2)}) %collective-permute-start.9) | collective-permute-done | bytes 259232 | tf_op jit(solution)/shard_map/ppermute | solution.py:155
  104.2 1.5 %fusion.30 = f32[2,2,45,360]{3,2,1,0:T(8,128)S(1)} fusion(f32[2,2,45,360]{3,2,1,0:T(8,128)} %collective-permute-done.9, pred[]{:T(512)S(6)} %or.3, s32[]{:T(128)S(6)} %select_n.89, f32[2,1,90,720]{3,2,1,0:T(8,128)S(1)} %get-tuple-element.61, f32[2,1,90,720]{3,2,1,0:T(8,128)S(1)} %get-tuple-element.60, s32[90]{0:T(128)S(1)} %dynamic_slice.11, ...), kind=kOutput, calls=%fused_computation.41 | convolution fusion | flops 70182448 | bytes 1555745 | tf_op jit(solution)/shard_map/sr,abrc->absc/dot_general | solution.py:149
  106.6 1.4 %fusion.29 = f32[2,90,1440]{2,1,0:T(8,128)S(1)} fusion(f32[1,90,1440]{2,1,0:T(8,128)S(1)} %copy-done.12, f32[1,90,1440]{2,1,0:T(8,128)} %get-tuple-element.30, f32[90,1440]{1,0:T(8,128)} %collective-permute-done.8, f32[90,1440]{1,0:T(8,128)S(1)} %copy-done.18), kind=kLoop, calls=%fused_computation.36 | loop fusion | flops 1036800 | bytes 3110400 | tf_op jit(solution)/shard_map/add | solution.py:174
  108.0 1.8 %copy.104 = f32[2,90,1440]{2,0,1:T(2,128)} copy(f32[2,90,1440]{2,1,0:T(8,128)S(1)} %fusion.29) | data formatting | bytes 2073600
  (109 shorter events, 25.7 us)
Async XLA Ops:
  2.1 19.4 %collective-permute-start = (f32[2,90,2]{2,1,0:T(8,128)S(1)}, f32[2,90,2]{2,1,0:T(8,128)S(1)}, u32[]{:S(2)}, u32[]{:S(2)}) collective-permute-start(f32[2,90,2]{2,1,0:T(8,128)S(1)} %copy.87), channel_id=1, source_target_pairs={{0,2},{2,0},{1,3},{3,1},{4,6},{6,4},{5,7},{7,5},{8,10},{10,8},{9,1... | collective-permute-start | bytes 4328 | tf_op jit(solution)/shard_map/ppermute | solution.py:22
  3.7 17.8 %collective-permute-start.1 = (f32[2,1,1440]{2,1,0:T(1,128)}, f32[2,1,1440]{2,1,0:T(1,128)}, u32[]{:S(2)}, u32[]{:S(2)}) collective-permute-start(f32[2,1,1440]{2,1,0:T(1,128)} %copy.92), channel_id=1, source_target_pairs={{4,0},{8,4},{12,8},{5,1},{9,5},{13,9},{6,2},{10,6},{14,10},{7,3},{... | collective-permute-start | bytes 34568 | tf_op jit(solution)/shard_map/ppermute | solution.py:28
  6.4 15.2 %collective-permute-start.2 = (f32[2,1,1440]{2,1,0:T(1,128)}, f32[2,1,1440]{2,1,0:T(1,128)}, u32[]{:S(2)}, u32[]{:S(2)}) collective-permute-start(f32[2,1,1440]{2,1,0:T(1,128)} %copy.93), channel_id=1, source_target_pairs={{0,4},{4,8},{8,12},{1,5},{5,9},{9,13},{2,6},{6,10},{10,14},{3,7},{... | collective-permute-start | bytes 34568 | tf_op jit(solution)/shard_map/ppermute | solution.py:28
  9.6 3.9 %copy-start.2 = (f32[2,90,1440]{2,0,1:T(2,128)S(1)}, f32[2,90,1440]{2,0,1:T(2,128)}, u32[]{:S(2)}) copy-start(f32[2,90,1440]{2,0,1:T(2,128)} %param.15) | copy-start | bytes 3110404
  13.6 3.8 %copy-start.19 = (f32[24,360]{1,0:T(8,128)S(1)}, f32[24,360]{1,0:T(8,128)}, u32[]{:S(2)}) copy-start(f32[24,360]{1,0:T(8,128)} %constant.102.clone) | copy-start | bytes 103684
  17.3 1.6 %copy-start.6 = (f32[2,90,1439]{2,0,1:T(2,128)S(1)}, f32[2,90,1439]{2,0,1:T(2,128)}, u32[]{:S(2)}) copy-start(f32[2,90,1439]{2,0,1:T(2,128)} %get-tuple-element.49) | copy-start | bytes 3108244
  18.9 9.0 %copy-start = (f32[60,24,360]{2,1,0:T(8,128)}, f32[60,24,360]{2,1,0:T(8,128)S(1)}, u32[]{:S(2)}) copy-start(f32[60,24,360]{2,1,0:T(8,128)S(1)} %get-tuple-element.65) | copy-start | bytes 6220804
  19.2 1.7 %copy-start.8 = (f32[2,89,1440]{2,0,1:T(2,128)S(1)}, f32[2,89,1440]{2,0,1:T(2,128)}, u32[]{:S(2)}) copy-start(f32[2,89,1440]{2,0,1:T(2,128)} %get-tuple-element.47) | copy-start | bytes 3075844
  19.4 1.8 %copy-start.7 = (f32[2,89,1440]{2,0,1:T(2,128)S(1)}, f32[2,89,1440]{2,0,1:T(2,128)}, u32[]{:S(2)}) copy-start(f32[2,89,1440]{2,0,1:T(2,128)} %get-tuple-element.46) | copy-start | bytes 3075844
  31.1 1.7 %copy-start.11 = (f32[180,360]{1,0:T(8,128)}, f32[180,360]{1,0:T(8,128)S(1)}, u32[]{:S(2)}) copy-start(f32[180,360]{1,0:T(8,128)S(1)} %get-tuple-element.73) | copy-start | bytes 777604
  31.1 6.3 %copy-start.27 = (s32[180]{0:T(256)S(1)}, s32[180]{0:T(256)}, u32[]{:S(2)}) copy-start(s32[180]{0:T(256)} %param.18) | copy-start | bytes 2164
  31.1 6.3 %copy-start.28 = (s32[180]{0:T(256)S(1)}, s32[180]{0:T(256)}, u32[]{:S(2)}) copy-start(s32[180]{0:T(256)} %param.19) | copy-start | bytes 2164
  31.1 6.4 %copy-start.20 = (s32[720]{0:T(1024)S(1)}, s32[720]{0:T(1024)}, u32[]{:S(2)}) copy-start(s32[720]{0:T(1024)} %add_select_fusion) | copy-start | bytes 8644
  31.1 6.4 %copy-start.21 = (f32[720]{0:T(1024)S(1)}, f32[720]{0:T(1024)}, u32[]{:S(2)}) copy-start(f32[720]{0:T(1024)} %select_multiply_fusion) | copy-start | bytes 8644
  32.8 13.2 %collective-permute-start.3 = (f32[180,720]{1,0:T(8,128)}, f32[180,720]{1,0:T(8,128)}, u32[]{:S(2)}, u32[]{:S(2)}) collective-permute-start(f32[180,720]{1,0:T(8,128)} %pad_maximum_fusion.6), channel_id=1, source_target_pairs={{0,2},{2,0},{1,3},{3,1},{4,6},{6,4},{5,7},{7,5},{8,10},{10,8},{9,1... | collective-permute-start | bytes 1555208 | tf_op jit(solution)/shard_map/ppermute | solution.py:123
  36.6 21.5 %collective-permute-start.4 = (f32[180,720]{1,0:T(8,128)}, f32[180,720]{1,0:T(8,128)}, u32[]{:S(2)}, u32[]{:S(2)}) collective-permute-start(f32[180,720]{1,0:T(8,128)} %pad_maximum_fusion.7), channel_id=1, source_target_pairs={{0,2},{2,0},{1,3},{3,1},{4,6},{6,4},{5,7},{7,5},{8,10},{10,8},{9,1... | collective-permute-start | bytes 1555208 | tf_op jit(solution)/shard_map/ppermute | solution.py:123
  69.8 2.5 %copy-start.4 = (f32[2,90,1440]{2,1,0:T(8,128)S(1)}, f32[2,90,1440]{2,1,0:T(8,128)}, u32[]{:S(2)}) copy-start(f32[2,90,1440]{2,1,0:T(8,128)} %copy-done.3) | copy-start | bytes 3110404
  74.4 7.6 %copy-start.9 = (f32[90,720]{1,0:T(8,128)S(1)}, f32[90,720]{1,0:T(8,128)}, u32[]{:S(2)}) copy-start(f32[90,720]{1,0:T(8,128)} %compare_select_fusion) | copy-start | bytes 777604
  74.4 7.6 %copy-start.13 = (f32[2,1,90,720]{3,2,0,1:T(8,128)S(1)}, f32[2,1,90,720]{3,2,0,1:T(8,128)}, u32[]{:S(2)}) copy-start(f32[2,1,90,720]{3,2,0,1:T(8,128)} %reshape.203) | copy-start | bytes 1555204
  74.4 7.6 %copy-start.14 = (f32[2,1,90,720]{3,2,0,1:T(8,128)S(1)}, f32[2,1,90,720]{3,2,0,1:T(8,128)}, u32[]{:S(2)}) copy-start(f32[2,1,90,720]{3,2,0,1:T(8,128)} %reshape.204) | copy-start | bytes 1555204
  74.8 7.3 %collective-permute-start.5 = (f32[2,90,2]{2,1,0:T(8,128)S(1)}, f32[2,90,2]{2,1,0:T(8,128)S(1)}, u32[]{:S(2)}, u32[]{:S(2)}) collective-permute-start(f32[2,90,2]{2,1,0:T(8,128)S(1)} %pad_maximum_fusion.8), channel_id=1, source_target_pairs={{0,2},{2,0},{1,3},{3,1},{4,6},{6,4},{5,7},{7,5},{8,10},{10,8},{9,1... | collective-permute-start | bytes 4328 | tf_op jit(solution)/shard_map/ppermute | solution.py:22
  76.1 6.1 %collective-permute-start.6 = (f32[2,1,1440]{2,1,0:T(1,128)S(1)}, f32[2,1,1440]{2,1,0:T(1,128)S(1)}, u32[]{:S(2)}, u32[]{:S(2)}) collective-permute-start(f32[2,1,1440]{2,1,0:T(1,128)S(1)} %get-tuple-element.33), channel_id=1, source_target_pairs={{4,0},{8,4},{12,8},{5,1},{9,5},{13,9},{6,2},{10,6},{14,10},{7,3},{... | collective-permute-start | bytes 34568 | tf_op jit(solution)/shard_map/ppermute | solution.py:28
  78.8 4.6 %copy-start.15 = (f32[2,90,1440]{2,0,1:T(2,128)S(1)}, f32[2,90,1440]{2,0,1:T(2,128)}, u32[]{:S(2)}) copy-start(f32[2,90,1440]{2,0,1:T(2,128)} %param.14) | copy-start | bytes 3110404
  78.8 4.6 %copy-start.23 = (f32[2]{0:T(128)S(1)}, f32[2]{0:T(128)}, u32[]{:S(2)}) copy-start(f32[2]{0:T(128)} %param.17) | copy-start | bytes 28
  78.8 4.6 %copy-start.24 = (f32[90]{0:T(128)S(1)}, f32[90]{0:T(128)}, u32[]{:S(2)}) copy-start(f32[90]{0:T(128)} %broadcast_divide_fusion) | copy-start | bytes 1084
  78.8 4.6 %collective-permute-start.7 = (f32[2,1,1440]{2,1,0:T(1,128)S(1)}, f32[2,1,1440]{2,1,0:T(1,128)S(1)}, u32[]{:S(2)}, u32[]{:S(2)}) collective-permute-start(f32[2,1,1440]{2,1,0:T(1,128)S(1)} %get-tuple-element.32), channel_id=1, source_target_pairs={{0,4},{4,8},{8,12},{1,5},{5,9},{9,13},{2,6},{6,10},{10,14},{3,7},{... | collective-permute-start | bytes 34568 | tf_op jit(solution)/shard_map/ppermute | solution.py:28
  84.2 7.9 %copy-start.25 = (s32[45]{0:T(128)S(1)}, s32[45]{0:T(128)}, u32[]{:S(2)}) copy-start(s32[45]{0:T(128)} %iota_add_fusion) | copy-start | bytes 544
  85.3 21.2 %collective-permute-start.8 = (f32[90,1440]{1,0:T(8,128)}, f32[90,1440]{1,0:T(8,128)}, u32[]{:S(2)}, u32[]{:S(2)}) collective-permute-start(f32[90,1440]{1,0:T(8,128)} %bitcast.11), channel_id=1, source_target_pairs={{1,0},{3,2},{5,4},{7,6},{9,8},{11,10},{13,12},{15,14},{17,16},{19,... | collective-permute-start | bytes 1555208 | tf_op jit(solution)/shard_map/ppermute | solution.py:171
  93.4 10.9 %collective-permute-start.9 = (f32[2,2,45,360]{3,2,1,0:T(8,128)}, f32[2,2,45,360]{3,2,1,0:T(8,128)}, u32[]{:S(2)}, u32[]{:S(2)}) collective-permute-start(f32[2,2,45,360]{3,2,1,0:T(8,128)} %convolution_bitcast_fusion), channel_id=1, source_target_pairs={{12,4},{0,8},{13,5},{1,9},{14,6},{2,10},{15,7},{3,11},{28,20},{16,... | collective-permute-start | bytes 777608 | tf_op jit(solution)/shard_map/ppermute | solution.py:155
  94.7 1.9 %copy-start.5 = (f32[2,90,1440]{2,1,0:T(8,128)S(1)}, f32[2,90,1440]{2,1,0:T(8,128)}, u32[]{:S(2)}) copy-start(f32[2,90,1440]{2,1,0:T(8,128)} %get-tuple-element.26) | copy-start | bytes 3110404
  100.2 6.4 %copy-start.12 = (f32[1,90,1440]{2,1,0:T(8,128)S(1)}, f32[1,90,1440]{2,1,0:T(8,128)}, u32[]{:S(2)}) copy-start(f32[1,90,1440]{2,1,0:T(8,128)} %get-tuple-element.31) | copy-start | bytes 1555204
  100.2 6.4 %copy-start.18 = (f32[90,1440]{1,0:T(8,128)S(1)}, f32[90,1440]{1,0:T(8,128)}, u32[]{:S(2)}) copy-start(f32[90,1440]{1,0:T(8,128)} %param.16) | copy-start | bytes 1555204
  (7 other events, 9.3 us)
where the time goes:
time: 111 us; the launch traced here: 110 us
  local copies, waits for them, and re-layouts  33.2 us (30%)
  other arithmetic  22.3 us (20%)
  starting transfers between devices  22.3 us (20%)
  waiting for transfers between devices  18.8 us (17%)
  matrix products  12.2 us (11%)
  between operations  1.14 us (1%)
    unnamed x69, local copies, waits for them, and re-layouts  15.2 us
    ppermute x2, waiting for transfers between devices, local(): sums = part + lax.ppermute(part, 'lon', [(0, 1), (1, 0)])  13.6 us
    reshape x4, local copies, waits for them, and re-layouts, local(): both_sums.append(sums.reshape(2, lat_dev, 2 * KMAX) * factor[None])  7.7 us
    ppermute x1, starting transfers between devices, local(): lax.ppermute(columns[0], 'lev', [(i + distance, i) for i in range(lev_cou...  6.81 us
    slice x4, local copies, waits for them, and re-layouts, diff(): lax.slice_in_dim(block, 0, size - 1, axis=dim)  6.48 us
    ppermute x2, starting transfers between devices, edges(): lax.ppermute(last, axis, forward)  6.4 us
    dot_general x2, matrix products, local(): lax.dot_general(turned_back.reshape(2 * lat_dev, 2 * KMAX), basis, (((1,)...  5.13 us
    ppermute x2, starting transfers between devices, edges(): lax.ppermute(first, axis, backward)  4.7 us
  transfers between devices with their start and end apart: 10, of which 4 were waited for; matrix products, arithmetic and copies ran while one was open for 29% of the time, Pallas kernels for 0%

commit v1 on v0

--- a/solution.py
+++ b/solution.py
@@ -1,9 +1,13 @@
 import math
+
+import functools
 
 import jax
 import numpy as np
 import jax.numpy as jnp
 from jax import lax
+from jax.experimental import pallas as pl
+from jax.experimental.pallas import tpu as pltpu
 from jax.sharding import PartitionSpec as P
 
 KMAX = 360
@@ -175,9 +179,362 @@
     return (east_final, north_final, thick_new, geo_new, spectra)
 
 
+FINE = 32
+
+
+def angle_tables(count, nlon_total):
+    k = np.arange(KMAX, dtype=np.int64)[None, :]
+    angle = 2.0 * np.pi / nlon_total
+
+    def table(columns):
+        phase = (columns[:, None] * k % nlon_total) * angle
+        return np.cos(phase), np.sin(phase)
+
+    cc, cs = table(np.arange(0, count, FINE))
+    fc, fs = table(np.arange(FINE))
+    coarse = np.stack([np.concatenate([cc, cs], 1), np.concatenate([-cs, cc], 1)])
+    fine = np.stack([np.concatenate([fc, fc], 1), np.concatenate([fs, fs], 1)])
+    return coarse.astype(np.float32), fine.astype(np.float32)
+
+
+def split(x):
+    high = x.astype(jnp.bfloat16)
+    return high, (x - high.astype(jnp.float32)).astype(jnp.bfloat16)
+
+
+def three_pass(x, high_ref, low_ref, dims):
+    high, low = split(x)
+    rows = x.shape[0]
+
+    def dot(a, b):
+        return lax.dot_general(a, b, (dims, ((), ())), preferred_element_type=jnp.float32)
+
+    basis = high_ref[...]
+    return dot(high, basis) + dot(low, basis) + dot(high, low_ref[...])
+
+
+def substep_kernel(
+    sizes,
+    depth_ref, kept_ref, slot_ref, row_ref, coarse_ref, fine_ref,
+    we_hbm, wn_hbm, th_hbm, geo_hbm, sg_hbm,
+    east_out, north_out, thick_out, geo_out, spectra_out,
+    we, wn, th, geo, sg, rows_ref, high_ref, low_ref, part, came,
+    lon_put, lon_got, lat_put, lat_got, column_put, column_got, spec_put, spec_got,
+    in_sem, lon_sem, lat_sem, part_sem, column_sem, spec_sem,
+):
+    lat_count, polar_bands, half_axis, nlon_total, north_coef = sizes
+    lev_dev, lat_dev, lon_dev = we.shape
+    help_rows = spec_put.shape[1]
+    lon = lax.axis_index("lon")
+    lat = lax.axis_index("lat")
+    lev = lax.axis_index("lev")
+    other_lon = {"lon": 1 - lon}
+    other_lev = {"lev": 1 - lev}
+    partner = lax.rem(lat + half_axis, lat_count)
+    far = {"lat": partner}
+    has_south = lat > 0
+    has_north = lat < lat_count - 1
+    polar = (lat < polar_bands) | (lat >= lat_count - polar_bands)
+    MESH = pl.DeviceIdType.MESH
+
+    loads = [
+        pltpu.make_async_copy(src, dst, in_sem.at[i])
+        for i, (src, dst) in enumerate(
+            ((geo_hbm, geo), (we_hbm, we), (wn_hbm, wn), (th_hbm, th), (sg_hbm, sg))
+        )
+    ]
+    for load in loads:
+        load.start()
+
+    barrier = pltpu.get_barrier_semaphore()
+    for target in (other_lon, other_lev, far):
+        pl.semaphore_signal(barrier, inc=1, device_id=target, device_id_type=MESH)
+
+    @pl.when(has_south)
+    def _():
+        pl.semaphore_signal(barrier, inc=1, device_id={"lat": lat - 1}, device_id_type=MESH)
+
+    @pl.when(has_north)
+    def _():
+        pl.semaphore_signal(barrier, inc=1, device_id={"lat": lat + 1}, device_id_type=MESH)
+
+    pl.semaphore_wait(barrier, 3 + has_south.astype(jnp.int32) + has_north.astype(jnp.int32))
+
+    def remote(src, dst, sems, target):
+        return pltpu.make_async_remote_copy(
+            src_ref=src, dst_ref=dst, send_sem=sems.at[0], recv_sem=sems.at[1],
+            device_id=target, device_id_type=MESH,
+        )
+
+    lane = lax.broadcasted_iota(jnp.int32, (lat_dev, lon_dev), 1)
+    row = lax.broadcasted_iota(jnp.int32, (lat_dev, lon_dev), 0)
+    edge_lane = lax.broadcasted_iota(jnp.int32, (lat_dev, 128), 1)
+
+    def send_lon(turn, field):
+        held = jnp.zeros((lat_dev, 128), jnp.float32)
+        for level in range(lev_dev):
+            held = jnp.where(edge_lane == 2 * level, field[level, :, 0:1], held)
+            held = jnp.where(edge_lane == 2 * level + 1, field[level, :, lon_dev - 1 : lon_dev], held)
+        lon_put[turn, :, 0:lat_dev] = jnp.transpose(held)[0:8]
+        copy = remote(lon_put.at[turn], lon_got.at[turn], lon_sem.at[turn], other_lon)
+        copy.start()
+        return copy
+
+    def send_lat(turn, field, scale):
+        for level in range(lev_dev):
+            lat_put[turn, 0, level : level + 1, :] = field[level, 0:1, :] * scale[0:1]
+            lat_put[turn, 1, level : level + 1, :] = (
+                field[level, lat_dev - 1 : lat_dev, :] * scale[lat_dev - 1 : lat_dev]
+            )
+        south = remote(lat_put.at[turn, 0], lat_got.at[turn, 1], lat_sem.at[turn, 0], {"lat": lat - 1})
+        north = remote(lat_put.at[turn, 1], lat_got.at[turn, 0], lat_sem.at[turn, 1], {"lat": lat + 1})
+
+        @pl.when(has_south)
+        def _():
+            south.start()
+
+        @pl.when(has_north)
+        def _():
+            north.start()
+
+        @pl.when(jnp.logical_not(has_south))
+        def _():
+            lat_got[turn, 0] = jnp.zeros_like(lat_got[turn, 0])
+
+        @pl.when(jnp.logical_not(has_north))
+        def _():
+            lat_got[turn, 1] = jnp.zeros_like(lat_got[turn, 1])
+
+        return south, north
+
+    def wait_lat(south, north):
+        @pl.when(has_south)
+        def _():
+            south.wait_send()
+            north.wait_recv()
+
+        @pl.when(has_north)
+        def _():
+            north.wait_send()
+            south.wait_recv()
+
+    def east_diff(x, turn, level, rims):
+        first = rims[:, 2 * level : 2 * level + 1]
+        last = rims[:, 2 * level + 1 : 2 * level + 2]
+        up = jnp.where(lane == lon_dev - 1, first, pltpu.roll(x, lon_dev - 1, 1))
+        down = jnp.where(lane == 0, last, pltpu.roll(x, 1, 1))
+        return up - down
+
+    def north_diff(x, turn, level):
+        up = jnp.concatenate([x[1:], lat_got[turn, 1, level : level + 1, :]], axis=0)
+        down = jnp.concatenate([lat_got[turn, 0, level : level + 1, :], x[:-1]], axis=0)
+        return up - down
+
+    cos_lat = row_ref[:, 0:1]
+    sin_lat = row_ref[:, 1:2]
+    east_coef = row_ref[:, 2:3]
+    flux_coef = row_ref[:, 3:4]
+    one = jnp.ones((lat_dev, 1), jnp.float32)
+
+    loads[0].wait()
+    lon_copy = send_lon(0, geo)
+    lat_copies = send_lat(0, geo, one)
+
+    def make_basis(block, _):
+        p = coarse_ref[0, pl.ds(block, 1), :]
+        q = coarse_ref[1, pl.ds(block, 1), :]
+        values = p * fine_ref[0] + q * fine_ref[1]
+        high, low = split(values)
+        at = pl.ds(pl.multiple_of(block * FINE, FINE), FINE)
+        high_ref[at, :] = high
+        low_ref[at, :] = low
+        return _
+
+    lax.fori_loop(0, lon_dev // FINE, make_basis, 0)
+    for load in loads[1:]:
+        load.wait()
+    lon_copy.wait()
+    wait_lat(*lat_copies)
+
+    rims = jnp.transpose(lon_got[0])[0:lat_dev]
+    part_copies = []
+    for level in range(lev_dev):
+        x = geo[level]
+        east = we[level]
+        north = wn[level]
+        east_new = east - east_coef * east_diff(x, 0, level, rims) + CORIOLIS * sin_lat * north
+        north_new = north - north_coef * north_diff(x, 0, level) - CORIOLIS * sin_lat * east
+        rows_ref[level, 0:lat_dev, :] = east_new
+        rows_ref[level, lat_dev:, :] = north_new
+        east_out[level] = east_new
+        north_out[level] = north_new
+        part[level] = three_pass(rows_ref[level], high_ref, low_ref, ((1,), (0,)))
+        copy = remote(part.at[level], came.at[level], part_sem.at[level], other_lon)
+        copy.start()
+        part_copies.append(copy)
+
+    column_id = lax.broadcasted_iota(jnp.int32, (lat_dev, 2 * KMAX), 1)
+    wavenumber = jnp.where(column_id < KMAX, column_id, column_id - KMAX)
+    weight = jnp.where(wavenumber == 0, 1.0 / nlon_total, 2.0 / nlon_total)
+    odd = 1.0 - 2.0 * lax.rem(wavenumber, 2).astype(jnp.float32)
+    first = jnp.where(lat < polar_bands, lat, jnp.maximum(lat - (lat_count - 2 * polar_bands), 0))
+    first = jnp.minimum(first, 2 * polar_bands - 1)
+    kept = kept_ref[first]
+    slots = slot_ref[first]
+    factor = jnp.where(wavenumber < kept, weight, 0.0)
+    factor2 = jnp.concatenate([factor, factor], axis=0)
+    odd_row = odd[0:1]
+    for level in range(lev_dev):
+        part_copies[level].wait()
+        kept_sums = (part[level] + odd_row * came[level]) * factor2
+        came[level] = kept_sums
+        filtered = three_pass(kept_sums, high_ref, low_ref, ((1,), (1,)))
+
+        @pl.when(polar)
+        def _():
+            east_out[level] = filtered[0:lat_dev]
+            north_out[level] = filtered[lat_dev:]
+
+    lon_copy = send_lon(1, east_out)
+    lat_copies = send_lat(1, north_out, cos_lat)
+
+    place = lax.broadcasted_iota(jnp.int32, (lat_dev, help_rows), 1)
+    match_own = (slots == lat * help_rows + place).astype(jnp.float32)
+    match_far = (slots == partner * help_rows + place).astype(jnp.float32)
+
+    def gathered(match, level, wind):
+        values = came[level, wind * lat_dev : (wind + 1) * lat_dev, :]
+        picked = lax.dot_general(
+            match, values, (((0,), (0,)), ((), ())),
+            precision=lax.Precision.HIGHEST, preferred_element_type=jnp.float32,
+        )
+        spun = picked * odd[0:help_rows]
+        return jnp.where(lon == 0, picked[:, 0:KMAX], spun[:, KMAX:])
+
+    spec_copy = remote(spec_put, spec_got, spec_sem, far)
+
+    @pl.when(polar)
+    def _():
+        for wind in range(2):
+            for level in range(lev_dev):
+                spec_put[wind * lev_dev + level] = gathered(match_far, level, wind)
+        spec_copy.start()
+        for wind in range(2):
+            for level in range(lev_dev):
+                spectra_out[wind, level] = gathered(match_own, level, wind)
+
+    lon_copy.wait()
+    wait_lat(*lat_copies)
+    rims = jnp.transpose(lon_got[1])[0:lat_dev]
+    below = None
+    for level in range(lev_dev - 1, -1, -1):
+        flux = north_out[level] * cos_lat
+        divergence = east_coef * east_diff(east_out[level], 1, level, rims) + flux_coef * north_diff(
+            flux, 1, level
+        )
+        thick = th[level] - depth_ref[level] * divergence
+        thick_out[level] = thick
+        below = thick if below is None else below + thick
+        geo_out[level] = below
+    column_put[...] = below
+    column_copy = remote(column_put, column_got, column_sem, other_lev)
+
+    @pl.when(lev == 1)
+    def _():
+        column_copy.start()
+        for level in range(lev_dev):
+            geo_out[level] = sg[...] + GRAVITY * geo_out[level]
+
+    @pl.when(lev == 0)
+    def _():
+        column_copy.wait_recv()
+        for level in range(lev_dev):
+            geo_out[level] = sg[...] + GRAVITY * (geo_out[level] + column_got[...])
+
+    @pl.when(lev == 1)
+    def _():
+        column_copy.wait_send()
+
+    @pl.when(polar)
+    def _():
+        spec_copy.wait_send()
+
+    @pl.when(jnp.logical_not(polar))
+    def _():
+        spec_copy.wait_recv()
+        for wind in range(2):
+            for level in range(lev_dev):
+                spectra_out[wind, level] = spec_got[wind * lev_dev + level]
+
+
+def one_kernel(
+    wind_east, wind_north, thickness, geopot, surface_geopot, mean_depth, kept_modes, slot_table
+):
+    lev_dev, lat_dev, lon_dev = thickness.shape
+    lat_count = lax.axis_size("lat")
+    nlat_total = lat_dev * lat_count
+    nlon_total = 2 * lon_dev
+    help_rows = lat_dev // 2
+    lam_step = 2.0 * math.pi / nlon_total
+    phi_step = math.pi / nlat_total
+    north_coef = STEP_FACTOR * lam_step / phi_step
+    global_rows = lax.axis_index("lat") * lat_dev + jnp.arange(lat_dev, dtype=jnp.int32)
+    latitude = -0.5 * math.pi + (global_rows.astype(jnp.float32) + 0.5) * phi_step
+    coslat = jnp.cos(latitude)
+    row_table = jnp.stack(
+        [coslat, jnp.sin(latitude), STEP_FACTOR / coslat, north_coef / coslat], axis=1
+    )
+    bands = 2 * (lat_count // 4)
+    coarse, fine = angle_tables(lon_dev, nlon_total)
+    whole = pl.BlockSpec(memory_space=pltpu.VMEM)
+    away = pl.BlockSpec(memory_space=pl.ANY)
+    field = jax.ShapeDtypeStruct((lev_dev, lat_dev, lon_dev), jnp.float32)
+    block = pltpu.VMEM((lev_dev, lat_dev, lon_dev), jnp.float32)
+    basis = pltpu.VMEM((lon_dev, 2 * KMAX), jnp.bfloat16)
+    sums = pltpu.VMEM((lev_dev, 2 * lat_dev, 2 * KMAX), jnp.float32)
+    specs = pltpu.VMEM((2 * lev_dev, help_rows, KMAX), jnp.float32)
+    dma = pltpu.SemaphoreType.DMA
+    return pl.pallas_call(
+        functools.partial(
+            substep_kernel,
+            (lat_count, lat_count // 4, lat_count // 2, nlon_total, north_coef),
+        ),
+        out_shape=(field,) * 4
+        + (jax.ShapeDtypeStruct((2, lev_dev, help_rows, KMAX), jnp.float32),),
+        in_specs=[pl.BlockSpec(memory_space=pltpu.SMEM)] + [whole] * 5 + [away] * 5,
+        out_specs=(whole,) * 5,
+        scratch_shapes=[
+            block, block, block, block,
+            pltpu.VMEM((lat_dev, lon_dev), jnp.float32),
+            pltpu.VMEM((lev_dev, 2 * lat_dev, lon_dev), jnp.float32),
+            basis, basis, sums, sums,
+            pltpu.VMEM((2, 8, 128), jnp.float32),
+            pltpu.VMEM((2, 8, 128), jnp.float32),
+            pltpu.VMEM((2, 2, lev_dev, lon_dev), jnp.float32),
+            pltpu.VMEM((2, 2, lev_dev, lon_dev), jnp.float32),
+            pltpu.VMEM((lat_dev, lon_dev), jnp.float32),
+            pltpu.VMEM((lat_dev, lon_dev), jnp.float32),
+            specs, specs,
+            dma((5,)), dma((2, 2)), dma((2, 2, 2)), dma((lev_dev, 2)), dma((2,)), dma((2,)),
+        ],
+        compiler_params=pltpu.CompilerParams(
+            collective_id=0, has_side_effects=True, vmem_limit_bytes=60 * 2**20
+        ),
+    )(
+        mean_depth,
+        kept_modes.reshape(bands, lat_dev, 1),
+        slot_table.reshape(bands, lat_dev, 1),
+        row_table,
+        jnp.asarray(coarse),
+        jnp.asarray(fine),
+        wind_east, wind_north, thickness, geopot, surface_geopot,
+    )
+
+
 def solution(mesh):
+    body = one_kernel if mesh.shape["lon"] == 2 and mesh.shape["lev"] == 2 else local
     return jax.shard_map(
-        local,
+        body,
         mesh=mesh,
         in_specs=(
             P(("members", "lev"), "lat", "lon"),

time: 111 us -> 70.2 us (0.63)
  the two profiles are of different devices: /device:TPU:15 before, /device:TPU:0 now
where the time goes in v1:
time: 70.2 us; the launch traced here: 69.8 us
  Pallas kernels  48.8 us (70%)
  local copies, waits for them, and re-layouts  20.2 us (29%)
    pallas_call x1, Pallas kernels, one_kernel(): pl.pallas_call(functools.partial(substep_kernel, (lat_count, lat_count //...  48.8 us
    pallas_call x5, local copies, waits for them, and re-layouts, one_kernel(): pl.pallas_call(functools.partial(substep_kernel, (lat_count, lat_count //...  9.6 us
    unnamed x18, local copies, waits for them, and re-layouts  6.76 us
    reshape x1, local copies, waits for them, and re-layouts, one_kernel(): slot_table.reshape(bands, lat_dev, 1)  1.62 us
    reshape x1, local copies, waits for them, and re-layouts, one_kernel(): kept_modes.reshape(bands, lat_dev, 1)  1.52 us

profile of v1, /device:TPU:0, one launch (start us, length us, event | category | flops | bytes accessed | tf_op | source)
XLA Modules:
  0.0 69.8 jit_solution(1099512470086997473)
XLA Ops:
  0.8 0.7 %copy.37.row_ref = f32[90,4]{1,0:T(8,128)} copy(f32[90,4]{0,1:T(4,128)S(1)} %pad_maximum_fusion) | data formatting | bytes 2880 | tf_op jit(solution)/shard_map/stack | solution.py:484
  1.5 1.5 %reshape.52.kept_ref = s32[2,90,1]{2,1,0:T(8,128)} reshape(s32[180]{0:T(256)} %param.16) | data formatting | bytes 1440 | tf_op jit(solution)/shard_map/reshape | solution.py:525
  3.0 0.0 copy-start.3
  3.0 1.6 %reshape.53.slot_ref = s32[2,90,1]{2,1,0:T(8,128)} reshape(s32[180]{0:T(256)} %param.17) | data formatting | bytes 1440 | tf_op jit(solution)/shard_map/reshape | solution.py:526
  4.6 2.5 %copy.38.we_hbm = f32[2,90,1440]{2,1,0:T(8,128)} copy(f32[2,90,1440]{2,0,1:T(2,128)} %param.10) | data formatting | bytes 2073600 | tf_op args[0]
  7.1 0.0 copy-done.3
  7.1 0.0 copy-start.4
  7.1 1.2 %copy.39.wn_hbm = f32[2,90,1440]{2,1,0:T(8,128)} copy(f32[2,90,1440]{2,0,1:T(2,128)S(1)} %copy-done.3) | data formatting | bytes 2073600 | tf_op args[1]
  8.4 0.3 copy-done.4
  8.6 0.0 copy-start.5
  8.6 1.2 %copy.40.th_hbm = f32[2,90,1440]{2,1,0:T(8,128)} copy(f32[2,90,1440]{2,0,1:T(2,128)S(1)} %copy-done.4) | data formatting | bytes 2073600 | tf_op args[2]
  9.9 0.3 copy-done.5
  10.1 1.2 %copy.41.geo_hbm = f32[2,90,1440]{2,1,0:T(8,128)} copy(f32[2,90,1440]{2,0,1:T(2,128)S(1)} %copy-done.5) | data formatting | bytes 2073600 | tf_op args[3]
  11.4 48.8 %shard_map.137 = (f32[2,90,1440]{2,1,0:T(8,128)}, f32[2,90,1440]{2,1,0:T(8,128)}, f32[2,90,1440]{2,1,0:T(8,128)}, f32[2,90,1440]{2,1,0:T(8,128)}, f32[2,2,45,360]{3,2,1,0:T(8,128)}) custom-call(f32[2]{0:T(128)} %depth_ref.1, s32[2,90,1]{2,1,0:T(8,128)} %reshape.52.kept_ref, s32[2,90,1]{2,1,0:T(8,128)} %reshape.53.slot_ref, f32[90,4]{1,0:T(8,128)} %copy.37.row_ref, ...), custom_call_target="tpu_custom_call" | custom-call | tf_op jit(solution)/shard_map/pallas_call | solution.py:497
  60.2 0.0 copy-start.6
  60.2 0.0 copy-start.2
  60.2 3.2 %copy.42 = f32[2,90,1440]{2,0,1:T(2,128)} copy(f32[2,90,1440]{2,1,0:T(8,128)} %get-tuple-element.15) | data formatting | bytes 2073600 | tf_op jit(solution)/shard_map/pallas_call | solution.py:497
  63.4 0.0 copy-done.6
  63.4 0.8 %copy.46 = f32[2,2,45,360]{3,1,2,0:T(2,128)} copy(f32[2,2,45,360]{3,2,1,0:T(8,128)S(1)} %copy-done.6) | data formatting | bytes 518400 | tf_op jit(solution)/shard_map/pallas_call | solution.py:497
  64.3 0.0 copy-done.2
  64.3 0.0 copy-start.1
  64.3 1.8 %copy.43 = f32[2,90,1440]{2,0,1:T(2,128)} copy(f32[2,90,1440]{2,1,0:T(8,128)S(1)} %copy-done.2) | data formatting | bytes 2073600 | tf_op jit(solution)/shard_map/pallas_call | solution.py:497
  66.1 0.0 copy-done.1
  66.1 0.0 copy-start
  66.1 1.8 %copy.44 = f32[2,90,1440]{2,0,1:T(2,128)} copy(f32[2,90,1440]{2,1,0:T(8,128)S(1)} %copy-done.1) | data formatting | bytes 2073600 | tf_op jit(solution)/shard_map/pallas_call | solution.py:497
  68.0 0.0 copy-done
  68.0 1.8 %copy.45 = f32[2,90,1440]{2,0,1:T(2,128)} copy(f32[2,90,1440]{2,1,0:T(8,128)S(1)} %copy-done) | data formatting | bytes 2073600 | tf_op jit(solution)/shard_map/pallas_call | solution.py:497
  (3 shorter events, 0.1 us)
Async XLA Ops:
  3.0 4.1 %copy-start.3 = (f32[2,90,1440]{2,0,1:T(2,128)S(1)}, f32[2,90,1440]{2,0,1:T(2,128)}, u32[]{:S(2)}) copy-start(f32[2,90,1440]{2,0,1:T(2,128)} %param.11) | copy-start | bytes 3110404
  7.1 1.5 %copy-start.4 = (f32[2,90,1440]{2,0,1:T(2,128)S(1)}, f32[2,90,1440]{2,0,1:T(2,128)}, u32[]{:S(2)}) copy-start(f32[2,90,1440]{2,0,1:T(2,128)} %param.12) | copy-start | bytes 3110404
  8.6 1.5 %copy-start.5 = (f32[2,90,1440]{2,0,1:T(2,128)S(1)}, f32[2,90,1440]{2,0,1:T(2,128)}, u32[]{:S(2)}) copy-start(f32[2,90,1440]{2,0,1:T(2,128)} %param.13) | copy-start | bytes 3110404
  60.2 3.2 %copy-start.6 = (f32[2,2,45,360]{3,2,1,0:T(8,128)S(1)}, f32[2,2,45,360]{3,2,1,0:T(8,128)}, u32[]{:S(2)}) copy-start(f32[2,2,45,360]{3,2,1,0:T(8,128)} %get-tuple-element.19) | copy-start | bytes 777604
  60.2 4.1 %copy-start.2 = (f32[2,90,1440]{2,1,0:T(8,128)S(1)}, f32[2,90,1440]{2,1,0:T(8,128)}, u32[]{:S(2)}) copy-start(f32[2,90,1440]{2,1,0:T(8,128)} %get-tuple-element.16) | copy-start | bytes 3110404
  64.3 1.8 %copy-start.1 = (f32[2,90,1440]{2,1,0:T(8,128)S(1)}, f32[2,90,1440]{2,1,0:T(8,128)}, u32[]{:S(2)}) copy-start(f32[2,90,1440]{2,1,0:T(8,128)} %get-tuple-element.17) | copy-start | bytes 3110404
  66.1 1.8 %copy-start = (f32[2,90,1440]{2,1,0:T(8,128)S(1)}, f32[2,90,1440]{2,1,0:T(8,128)}, u32[]{:S(2)}) copy-start(f32[2,90,1440]{2,1,0:T(8,128)} %get-tuple-element.18) | copy-start | bytes 3110404

commit v2 on v1

--- a/solution.py
+++ b/solution.py
@@ -213,21 +213,29 @@
     return dot(high, basis) + dot(low, basis) + dot(high, low_ref[...])
 
 
+def shares(rows):
+    padded = -(-rows // 8) * 8
+    direct = padded * 2 // 3 // 8 * 8
+    middle = direct + (padded - direct) // 16 * 8
+    return direct, ((direct, middle - direct), (middle, padded - middle))
+
+
 def substep_kernel(
     sizes,
-    depth_ref, kept_ref, slot_ref, row_ref, coarse_ref, fine_ref,
+    depth_ref, kept_ref, slot_ref, coarse_ref, fine_ref,
     we_hbm, wn_hbm, th_hbm, geo_hbm, sg_hbm,
-    east_out, north_out, thick_out, geo_out, spectra_out,
-    we, wn, th, geo, sg, rows_ref, high_ref, low_ref, part, came,
-    lon_put, lon_got, lat_put, lat_got, column_put, column_got, spec_put, spec_got,
-    in_sem, lon_sem, lat_sem, part_sem, column_sem, spec_sem,
+    east_hbm, north_hbm, thick_hbm, geo_new_hbm, spectra_hbm,
+    we, wn, th, geo, sg, spectra_out, rows_ref, high_ref, low_ref, part, came,
+    lon_put, lon_got, lat_put, lat_got, column_put, column_got, spec_put, spec_got, table_ref, hop_in, hop_over,
+    in_sem, out_sem, lon_sem, lat_sem, part_sem, hop_sem, column_sem, spec_sem,
 ):
-    lat_count, polar_bands, half_axis, nlon_total, north_coef = sizes
+    lat_count, polar_bands, half_axis, nlon_total, phi_step, north_coef = sizes
     lev_dev, lat_dev, lon_dev = we.shape
     help_rows = spec_put.shape[1]
     lon = lax.axis_index("lon")
     lat = lax.axis_index("lat")
     lev = lax.axis_index("lev")
+    east_out, north_out, thick_out, geo_out = we, wn, th, geo
     other_lon = {"lon": 1 - lon}
     other_lev = {"lev": 1 - lev}
     partner = lax.rem(lat + half_axis, lat_count)
@@ -238,11 +246,11 @@
     MESH = pl.DeviceIdType.MESH
 
     loads = [
-        pltpu.make_async_copy(src, dst, in_sem.at[i])
-        for i, (src, dst) in enumerate(
-            ((geo_hbm, geo), (we_hbm, we), (wn_hbm, wn), (th_hbm, th), (sg_hbm, sg))
-        )
+        pltpu.make_async_copy(src.at[:, level, :], dst.at[level], in_sem.at[i, level])
+        for i, (src, dst) in enumerate(((geo_hbm, geo), (we_hbm, we), (wn_hbm, wn), (th_hbm, th)))
+        for level in range(lev_dev)
     ]
+    loads.append(pltpu.make_async_copy(sg_hbm, sg, in_sem.at[4, 0]))
     for load in loads:
         load.start()
 
@@ -330,13 +338,16 @@
         down = jnp.concatenate([lat_got[turn, 0, level : level + 1, :], x[:-1]], axis=0)
         return up - down
 
-    cos_lat = row_ref[:, 0:1]
-    sin_lat = row_ref[:, 1:2]
-    east_coef = row_ref[:, 2:3]
-    flux_coef = row_ref[:, 3:4]
+    row_id = lax.broadcasted_iota(jnp.int32, (lat_dev, 1), 0) + lat * lat_dev
+    latitude = -0.5 * math.pi + (row_id.astype(jnp.float32) + 0.5) * phi_step
+    cos_lat = jnp.cos(latitude)
+    sin_lat = jnp.sin(latitude)
+    east_coef = STEP_FACTOR / cos_lat
+    flux_coef = north_coef / cos_lat
     one = jnp.ones((lat_dev, 1), jnp.float32)
 
-    loads[0].wait()
+    for load in loads[:lev_dev]:
+        load.wait()
     lon_copy = send_lon(0, geo)
     lat_copies = send_lat(0, geo, one)
 
@@ -350,28 +361,63 @@
         low_ref[at, :] = low
         return _
 
-    lax.fori_loop(0, lon_dev // FINE, make_basis, 0)
-    for load in loads[1:]:
+    @pl.when(polar)
+    def _():
+        lax.fori_loop(0, lon_dev // FINE, make_basis, 0)
+
+    for load in loads[lev_dev:]:
         load.wait()
     lon_copy.wait()
     wait_lat(*lat_copies)
 
     rims = jnp.transpose(lon_got[0])[0:lat_dev]
-    part_copies = []
+    next_band = {"lat": lat + 1 - 2 * lax.rem(lat, 2)}
+    rows = 2 * lat_dev
+    direct, chunks = shares(rows)
+    straight, hops = [], []
+    for level in range(lev_dev):
+        ahead = pl.ds(0, direct)
+        straight.append(
+            remote(part.at[level, ahead], came.at[level, ahead], part_sem.at[level], other_lon)
+        )
+        for chunk, (start, size) in enumerate(chunks):
+            full, held = pl.ds(start, size), pl.ds(start - direct, size)
+            hops.append(
+                (
+                    remote(part.at[level, full], hop_in.at[level, held], hop_sem.at[level, chunk, 0], next_band),
+                    remote(hop_in.at[level, held], hop_over.at[level, held], hop_sem.at[level, chunk, 1], other_lon),
+                    remote(hop_over.at[level, held], came.at[level, full], hop_sem.at[level, chunk, 2], next_band),
+                )
+            )
     for level in range(lev_dev):
         x = geo[level]
         east = we[level]
         north = wn[level]
         east_new = east - east_coef * east_diff(x, 0, level, rims) + CORIOLIS * sin_lat * north
         north_new = north - north_coef * north_diff(x, 0, level) - CORIOLIS * sin_lat * east
-        rows_ref[level, 0:lat_dev, :] = east_new
-        rows_ref[level, lat_dev:, :] = north_new
         east_out[level] = east_new
         north_out[level] = north_new
-        part[level] = three_pass(rows_ref[level], high_ref, low_ref, ((1,), (0,)))
-        copy = remote(part.at[level], came.at[level], part_sem.at[level], other_lon)
-        copy.start()
-        part_copies.append(copy)
+
+        @pl.when(polar)
+        def _():
+            rows_ref[level, 0:lat_dev, :] = east_new
+            rows_ref[level, lat_dev:, :] = north_new
+            part[level, 0:rows, :] = three_pass(rows_ref[level], high_ref, low_ref, ((1,), (0,)))
+            for out, _, _ in hops[level * len(chunks) : (level + 1) * len(chunks)]:
+                out.start()
+            straight[level].start()
+
+    @pl.when(jnp.logical_not(polar))
+    def _():
+        for out, over, _ in hops:
+            out.wait_recv()
+            over.start()
+        for _, over, back in hops:
+            over.wait_recv()
+            back.start()
+        for _, over, back in hops:
+            over.wait_send()
+            back.wait_send()
 
     column_id = lax.broadcasted_iota(jnp.int32, (lat_dev, 2 * KMAX), 1)
     wavenumber = jnp.where(column_id < KMAX, column_id, column_id - KMAX)
@@ -379,31 +425,54 @@
     odd = 1.0 - 2.0 * lax.rem(wavenumber, 2).astype(jnp.float32)
     first = jnp.where(lat < polar_bands, lat, jnp.maximum(lat - (lat_count - 2 * polar_bands), 0))
     first = jnp.minimum(first, 2 * polar_bands - 1)
-    kept = kept_ref[first]
-    slots = slot_ref[first]
+    table_ref[...] = jnp.zeros_like(table_ref)
+    for band in range(2 * polar_bands):
+        columns = slice(band * lat_dev, (band + 1) * lat_dev)
+
+        @pl.when(first == band)
+        def _():
+            table_ref[0:1, 0:lat_dev] = kept_ref[:, columns].astype(jnp.float32)
+            table_ref[1:2, 0:lat_dev] = slot_ref[:, columns].astype(jnp.float32)
+
+    table = jnp.transpose(table_ref[...])
+    kept = table[0:lat_dev, 0:1].astype(jnp.int32)
+    slots = table[0:lat_dev, 1:2].astype(jnp.int32)
     factor = jnp.where(wavenumber < kept, weight, 0.0)
     factor2 = jnp.concatenate([factor, factor], axis=0)
     odd_row = odd[0:1]
-    for level in range(lev_dev):
-        part_copies[level].wait()
-        kept_sums = (part[level] + odd_row * came[level]) * factor2
-        came[level] = kept_sums
-        filtered = three_pass(kept_sums, high_ref, low_ref, ((1,), (1,)))
-
-        @pl.when(polar)
-        def _():
+
+    @pl.when(polar)
+    def _():
+        for level in range(lev_dev):
+            straight[level].wait()
+            for out, _, back in hops[level * len(chunks) : (level + 1) * len(chunks)]:
+                out.wait_send()
+                back.wait_recv()
+            kept_sums = (part[level, 0:rows, :] + odd_row * came[level, 0:rows, :]) * factor2
+            part[level, 0:rows, :] = kept_sums
+            filtered = three_pass(kept_sums, high_ref, low_ref, ((1,), (1,)))
             east_out[level] = filtered[0:lat_dev]
             north_out[level] = filtered[lat_dev:]
 
     lon_copy = send_lon(1, east_out)
     lat_copies = send_lat(1, north_out, cos_lat)
+    stores = []
+
+    def store(index, src, dst):
+        for level in range(lev_dev):
+            copy = pltpu.make_async_copy(src.at[level], dst.at[:, level, :], out_sem.at[index, level])
+            copy.start()
+            stores.append(copy)
+
+    store(0, east_out, east_hbm)
+    store(1, north_out, north_hbm)
 
     place = lax.broadcasted_iota(jnp.int32, (lat_dev, help_rows), 1)
     match_own = (slots == lat * help_rows + place).astype(jnp.float32)
     match_far = (slots == partner * help_rows + place).astype(jnp.float32)
 
     def gathered(match, level, wind):
-        values = came[level, wind * lat_dev : (wind + 1) * lat_dev, :]
+        values = part[level, wind * lat_dev : (wind + 1) * lat_dev, :]
         picked = lax.dot_general(
             match, values, (((0,), (0,)), ((), ())),
             precision=lax.Precision.HIGHEST, preferred_element_type=jnp.float32,
@@ -436,6 +505,7 @@
         thick_out[level] = thick
         below = thick if below is None else below + thick
         geo_out[level] = below
+    store(2, thick_out, thick_hbm)
     column_put[...] = below
     column_copy = remote(column_put, column_got, column_sem, other_lev)
 
@@ -450,6 +520,8 @@
         column_copy.wait_recv()
         for level in range(lev_dev):
             geo_out[level] = sg[...] + GRAVITY * (geo_out[level] + column_got[...])
+
+    store(3, geo_out, geo_new_hbm)
 
     @pl.when(lev == 1)
     def _():
@@ -465,6 +537,18 @@
         for wind in range(2):
             for level in range(lev_dev):
                 spectra_out[wind, level] = spec_got[wind * lev_dev + level]
+
+    for wind in range(2):
+        for level in range(lev_dev):
+            copy = pltpu.make_async_copy(
+                spectra_out.at[wind, level],
+                spectra_hbm.at[wind, :, level, :],
+                out_sem.at[4, wind * lev_dev + level],
+            )
+            copy.start()
+            stores.append(copy)
+    for copy in stores:
+        copy.wait()
 
 
 def one_kernel(
@@ -478,34 +562,31 @@
     lam_step = 2.0 * math.pi / nlon_total
     phi_step = math.pi / nlat_total
     north_coef = STEP_FACTOR * lam_step / phi_step
-    global_rows = lax.axis_index("lat") * lat_dev + jnp.arange(lat_dev, dtype=jnp.int32)
-    latitude = -0.5 * math.pi + (global_rows.astype(jnp.float32) + 0.5) * phi_step
-    coslat = jnp.cos(latitude)
-    row_table = jnp.stack(
-        [coslat, jnp.sin(latitude), STEP_FACTOR / coslat, north_coef / coslat], axis=1
-    )
-    bands = 2 * (lat_count // 4)
     coarse, fine = angle_tables(lon_dev, nlon_total)
     whole = pl.BlockSpec(memory_space=pltpu.VMEM)
     away = pl.BlockSpec(memory_space=pl.ANY)
-    field = jax.ShapeDtypeStruct((lev_dev, lat_dev, lon_dev), jnp.float32)
+    field = jax.ShapeDtypeStruct((lat_dev, lev_dev, lon_dev), jnp.float32)
     block = pltpu.VMEM((lev_dev, lat_dev, lon_dev), jnp.float32)
     basis = pltpu.VMEM((lon_dev, 2 * KMAX), jnp.bfloat16)
-    sums = pltpu.VMEM((lev_dev, 2 * lat_dev, 2 * KMAX), jnp.float32)
+    padded_rows = -(-2 * lat_dev // 8) * 8
+    sums = pltpu.VMEM((lev_dev, padded_rows, 2 * KMAX), jnp.float32)
     specs = pltpu.VMEM((2 * lev_dev, help_rows, KMAX), jnp.float32)
     dma = pltpu.SemaphoreType.DMA
-    return pl.pallas_call(
+    direct, chunks = shares(2 * lat_dev)
+    hop = pltpu.VMEM((lev_dev, padded_rows - direct, 2 * KMAX), jnp.float32)
+    *fields, spectra = pl.pallas_call(
         functools.partial(
             substep_kernel,
-            (lat_count, lat_count // 4, lat_count // 2, nlon_total, north_coef),
+            (lat_count, lat_count // 4, lat_count // 2, nlon_total, phi_step, north_coef),
         ),
         out_shape=(field,) * 4
-        + (jax.ShapeDtypeStruct((2, lev_dev, help_rows, KMAX), jnp.float32),),
-        in_specs=[pl.BlockSpec(memory_space=pltpu.SMEM)] + [whole] * 5 + [away] * 5,
-        out_specs=(whole,) * 5,
+        + (jax.ShapeDtypeStruct((2, help_rows, lev_dev, KMAX), jnp.float32),),
+        in_specs=[pl.BlockSpec(memory_space=pltpu.SMEM)] + [whole] * 4 + [away] * 5,
+        out_specs=(away,) * 5,
         scratch_shapes=[
             block, block, block, block,
             pltpu.VMEM((lat_dev, lon_dev), jnp.float32),
+            pltpu.VMEM((2, lev_dev, help_rows, KMAX), jnp.float32),
             pltpu.VMEM((lev_dev, 2 * lat_dev, lon_dev), jnp.float32),
             basis, basis, sums, sums,
             pltpu.VMEM((2, 8, 128), jnp.float32),
@@ -515,24 +596,26 @@
             pltpu.VMEM((lat_dev, lon_dev), jnp.float32),
             pltpu.VMEM((lat_dev, lon_dev), jnp.float32),
             specs, specs,
-            dma((5,)), dma((2, 2)), dma((2, 2, 2)), dma((lev_dev, 2)), dma((2,)), dma((2,)),
+            pltpu.VMEM((8, 128), jnp.float32), hop, hop,
+            dma((5, lev_dev)), dma((5, 2 * lev_dev)), dma((2, 2)), dma((2, 2, 2)), dma((lev_dev, 2)), dma((lev_dev, len(chunks), 3, 2)), dma((2,)), dma((2,)),
         ],
         compiler_params=pltpu.CompilerParams(
             collective_id=0, has_side_effects=True, vmem_limit_bytes=60 * 2**20
         ),
     )(
         mean_depth,
-        kept_modes.reshape(bands, lat_dev, 1),
-        slot_table.reshape(bands, lat_dev, 1),
-        row_table,
+        kept_modes.reshape(1, -1),
+        slot_table.reshape(1, -1),
         jnp.asarray(coarse),
         jnp.asarray(fine),
-        wind_east, wind_north, thickness, geopot, surface_geopot,
+        *(jnp.transpose(x, (1, 0, 2)) for x in (wind_east, wind_north, thickness, geopot)),
+        surface_geopot,
     )
+    return (*(jnp.transpose(x, (1, 0, 2)) for x in fields), jnp.transpose(spectra, (0, 2, 1, 3)))
 
 
 def solution(mesh):
-    body = one_kernel if mesh.shape["lon"] == 2 and mesh.shape["lev"] == 2 else local
+    body = one_kernel if dict(mesh.shape, members=2) == dict(members=2, lat=4, lon=2, lev=2) else local
     return jax.shard_map(
         body,
         mesh=mesh,

time: 70.2 us -> 47.4 us (0.68)
  local copies, waits for them, and re-layouts: 20.2 us -> 7.51 us
  Pallas kernels: 48.8 us -> 38.9 us
    pallas_call x1, Pallas kernels: 48.8 us -> 38.9 us  [one_kernel(): pl.pallas_call(functools.partial(substep_kernel, (lat_count, lat_count //...]
    pallas_call x5 -> x0, local copies, waits for them, and re-layouts: 9.6 us -> none  [one_kernel(): pl.pallas_call(functools.partial(substep_kernel, (lat_count, lat_count //...]
    reshape x2 -> x0, local copies, waits for them, and re-layouts: 3.14 us -> none  [the longest x1 1.62 us: one_kernel(): slot_table.reshape(bands, lat_dev, 1)]
    unnamed x18 -> x13, local copies, waits for them, and re-layouts: 6.76 us -> 7.51 us
    another operation x1 -> x0, local copies, waits for them, and re-layouts: 0.73 us -> none  [one_kernel(): jnp.stack([coslat, jnp.sin(latitude), STEP_FACTOR / coslat, north_coef /...]
where the time goes in v2:
time: 47.4 us; the launch traced here: 47.1 us
  Pallas kernels  38.9 us (82%)
  local copies, waits for them, and re-layouts  7.51 us (16%)
  between operations  0.66 us (1%)
    pallas_call x1, Pallas kernels, one_kernel(): pl.pallas_call(functools.partial(substep_kernel, (lat_count, lat_count //...  38.9 us
    unnamed x13, local copies, waits for them, and re-layouts  7.51 us

profile of v2, /device:TPU:0, one launch (start us, length us, event | category | flops | bytes accessed | tf_op | source)
XLA Modules:
  0.0 47.1 jit_solution(15486125973983944245)
XLA Ops:
  0.6 38.9 %shard_map.137 = (f32[90,2,1440]{2,1,0:T(2,128)}, f32[90,2,1440]{2,1,0:T(2,128)}, f32[90,2,1440]{2,1,0:T(2,128)}, f32[90,2,1440]{2,1,0:T(2,128)}, f32[2,45,2,360]{3,2,1,0:T(2,128)}) custom-call(f32[2]{0:T(128)} %depth_ref.1, s32[1,180]{1,0:T(1,128)} %bitcast.20, s32[1,180]{1,0:T(1,128)} %bitcast.21, f32[2,45,720]{2,1,0:T(8,128)} %constant.4.clone.coarse_ref, ...), custom_call_target="tpu_custom_call" | custom-call | tf_op jit(solution)/shard_map/pallas_call | solution.py:577
  39.5 0.0 copy-start.2
  39.5 2.4 %copy.20 = f32[2,90,1440]{2,0,1:T(2,128)} copy(f32[2,90,1440]{2,0,1:T(2,128)} %bitcast.18) | data formatting | bytes 2073600
  41.9 0.0 copy-done.2
  41.9 0.0 copy-start.1
  41.9 1.0 %copy.21 = f32[2,90,1440]{2,0,1:T(2,128)} copy(f32[2,90,1440]{2,0,1:T(2,128)S(1)} %bitcast.17) | data formatting | bytes 2073600
  42.9 0.7 %copy-done.1 = f32[90,2,1440]{2,1,0:T(2,128)S(1)} copy-done((f32[90,2,1440]{2,1,0:T(2,128)S(1)}, f32[90,2,1440]{2,1,0:T(2,128)}, u32[]{:S(2)}) %copy-start.1) | copy-done | bytes 1036824
  43.6 0.0 copy-start
  43.6 1.0 %copy.22 = f32[2,90,1440]{2,0,1:T(2,128)} copy(f32[2,90,1440]{2,0,1:T(2,128)S(1)} %bitcast.16) | data formatting | bytes 2073600
  44.6 0.7 %copy-done = f32[90,2,1440]{2,1,0:T(2,128)S(1)} copy-done((f32[90,2,1440]{2,1,0:T(2,128)S(1)}, f32[90,2,1440]{2,1,0:T(2,128)}, u32[]{:S(2)}) %copy-start) | copy-done | bytes 1036824
  45.2 0.0 copy-start.3
  45.2 1.0 %copy.23 = f32[2,90,1440]{2,0,1:T(2,128)} copy(f32[2,90,1440]{2,0,1:T(2,128)S(1)} %bitcast.15) | data formatting | bytes 2073600
  46.2 0.1 copy-done.3
  46.4 0.7 %copy.24 = f32[2,2,45,360]{3,1,2,0:T(2,128)} copy(f32[2,2,45,360]{3,1,2,0:T(2,128)S(1)} %bitcast.19) | data formatting | bytes 518400
Async XLA Ops:
  39.5 2.4 %copy-start.2 = (f32[90,2,1440]{2,1,0:T(2,128)S(1)}, f32[90,2,1440]{2,1,0:T(2,128)}, u32[]{:S(2)}) copy-start(f32[90,2,1440]{2,1,0:T(2,128)} %get-tuple-element.11) | copy-start | bytes 3110404
  41.9 1.6 %copy-start.1 = (f32[90,2,1440]{2,1,0:T(2,128)S(1)}, f32[90,2,1440]{2,1,0:T(2,128)}, u32[]{:S(2)}) copy-start(f32[90,2,1440]{2,1,0:T(2,128)} %get-tuple-element.12) | copy-start | bytes 3110404
  43.6 1.6 %copy-start = (f32[90,2,1440]{2,1,0:T(2,128)S(1)}, f32[90,2,1440]{2,1,0:T(2,128)}, u32[]{:S(2)}) copy-start(f32[90,2,1440]{2,1,0:T(2,128)} %get-tuple-element.13) | copy-start | bytes 3110404
  45.2 1.1 %copy-start.3 = (f32[2,45,2,360]{3,2,1,0:T(2,128)S(1)}, f32[2,45,2,360]{3,2,1,0:T(2,128)}, u32[]{:S(2)}) copy-start(f32[2,45,2,360]{3,2,1,0:T(2,128)} %get-tuple-element.14) | copy-start | bytes 777604

commit v3 on v2

--- a/solution.py
+++ b/solution.py
@@ -180,6 +180,8 @@
 
 
 FINE = 32
+VMEM_MIB = 60
+STEPS = 5
 
 
 def angle_tables(count, nlon_total):
@@ -551,6 +553,28 @@
         copy.wait()
 
 
+def hand_on_kernel(*refs):
+    half = len(refs) // 2
+    for src, dst in zip(refs[:half], refs[half:]):
+        dst[...] = src[...]
+
+
+def handed_on(held):
+    def spec(x):
+        if x.ndim == 3:
+            return pl.BlockSpec((x.shape[0] // STEPS, *x.shape[1:]), lambda i: (i, 0, 0))
+        return pl.BlockSpec((x.shape[0], x.shape[1] // STEPS, *x.shape[2:]), lambda i: (0, i, 0, 0))
+
+    specs = [spec(x) for x in held]
+    return pl.pallas_call(
+        hand_on_kernel,
+        grid=(STEPS,),
+        out_shape=[jax.ShapeDtypeStruct(x.shape, x.dtype) for x in held],
+        in_specs=specs,
+        out_specs=specs,
+    )(*held)
+
+
 def one_kernel(
     wind_east, wind_north, thickness, geopot, surface_geopot, mean_depth, kept_modes, slot_table
 ):
@@ -574,7 +598,7 @@
     dma = pltpu.SemaphoreType.DMA
     direct, chunks = shares(2 * lat_dev)
     hop = pltpu.VMEM((lev_dev, padded_rows - direct, 2 * KMAX), jnp.float32)
-    *fields, spectra = pl.pallas_call(
+    held = pl.pallas_call(
         functools.partial(
             substep_kernel,
             (lat_count, lat_count // 4, lat_count // 2, nlon_total, phi_step, north_coef),
@@ -600,7 +624,7 @@
             dma((5, lev_dev)), dma((5, 2 * lev_dev)), dma((2, 2)), dma((2, 2, 2)), dma((lev_dev, 2)), dma((lev_dev, len(chunks), 3, 2)), dma((2,)), dma((2,)),
         ],
         compiler_params=pltpu.CompilerParams(
-            collective_id=0, has_side_effects=True, vmem_limit_bytes=60 * 2**20
+            collective_id=0, has_side_effects=True, vmem_limit_bytes=VMEM_MIB * 2**20
         ),
     )(
         mean_depth,
@@ -611,6 +635,7 @@
         *(jnp.transpose(x, (1, 0, 2)) for x in (wind_east, wind_north, thickness, geopot)),
         surface_geopot,
     )
+    *fields, spectra = handed_on(held)
     return (*(jnp.transpose(x, (1, 0, 2)) for x in fields), jnp.transpose(spectra, (0, 2, 1, 3)))
 
 

time: 47.4 us -> 45.9 us (0.968)
  local copies, waits for them, and re-layouts: 7.51 us -> 0 us
  Pallas kernels: 38.9 us -> 45 us
    unnamed x13 -> x0, local copies, waits for them, and re-layouts: 7.51 us -> none
    pallas_call x0 -> x1, Pallas kernels: none -> 6.12 us  [handed_on(): pl.pallas_call(hand_on_kernel, grid=(STEPS,), out_shape=[jax.ShapeDtypeSt...]
where the time goes in v3:
time: 45.9 us; the launch traced here: 45.6 us
  Pallas kernels  45 us (98%)
  between operations  0.64 us (1%)
    pallas_call x1, Pallas kernels, one_kernel(): pl.pallas_call(functools.partial(substep_kernel, (lat_count, lat_count //...  38.9 us
    pallas_call x1, Pallas kernels, handed_on(): pl.pallas_call(hand_on_kernel, grid=(STEPS,), out_shape=[jax.ShapeDtypeSt...  6.12 us

profile of v3, /device:TPU:0, one launch (start us, length us, event | category | flops | bytes accessed | tf_op | source)
XLA Modules:
  0.0 45.6 jit_solution(11069482794434421631)
XLA Ops:
  0.6 38.9 %shard_map.137 = (f32[90,2,1440]{2,1,0:T(2,128)}, f32[90,2,1440]{2,1,0:T(2,128)}, f32[90,2,1440]{2,1,0:T(2,128)}, f32[90,2,1440]{2,1,0:T(2,128)}, f32[2,45,2,360]{3,2,1,0:T(2,128)}) custom-call(f32[2]{0:T(128)} %depth_ref.1, s32[1,180]{1,0:T(1,128)} %bitcast.15, s32[1,180]{1,0:T(1,128)} %bitcast.16, f32[2,45,720]{2,1,0:T(8,128)} %constant.4.clone.coarse_ref, ...), custom_call_target="tpu_custom_call" | custom-call | tf_op jit(solution)/shard_map/pallas_call | solution.py:601
  39.5 6.1 %shard_map.138 = (f32[90,2,1440]{2,1,0:T(2,128)}, f32[90,2,1440]{2,1,0:T(2,128)}, f32[90,2,1440]{2,1,0:T(2,128)}, f32[90,2,1440]{2,1,0:T(2,128)}, f32[2,45,2,360]{3,2,1,0:T(2,128)}) custom-call(f32[90,2,1440]{2,1,0:T(2,128)} %get-tuple-element.15.refs_0_, f32[90,2,1440]{2,1,0:T(2,128)} %get-tuple-element.16.refs_1_, ...), custom_call_target="tpu_custom_call" | custom-call | tf_op jit(solution)/shard_map/pallas_call | solution.py:569
